TPU v7x, 256 devices: a whole 4x4x8 slice. The times are simulated.
256 devices in a mesh: ep: 64 (over z, y, core), sp: 4 (over x).
Axes of the slice: x: 4, y: 4, z: 8, core: 2. Of those that a mesh axis runs over, the one named last changes fastest.
Arguments:
- stream: bfloat16 [32768, 4096], P(('ep', 'sp')), may hold values from -30 to 30
- query_base: bfloat16 [32768, 4096], P(('ep', 'sp')), may hold values from -40 to 40
- key_heads: bfloat16 [32768, 1024], P(('ep', 'sp')), may hold values from -6 to 6
- value_heads: bfloat16 [32768, 1024], P(('ep', 'sp')), may hold values from -12 to 12
- attention_gain: bfloat16 [4096], replicated, may hold values from 0.099609375 to 1.8984375
- expert_gain: bfloat16 [4096], replicated, may hold values from 0.099609375 to 1.8984375
- adapter_down: bfloat16 [4096, 128], P('sp'), may hold values from -0.09375 to 0.09375
- adapter_up: bfloat16 [4096, 128], P('sp'), may hold values from -1 to 1
- user_index: int32 [64], P('ep'), may hold values from 0 to 3
- routes: int32 [32768, 2], P('ep'), may hold values from 0 to 63, all different within a row; in each aligned block of 128 rows (0 to 127, 128 to 255, ...) at most 5 rows name the same one
- route_weights: int32 [32768, 2], P(('ep', 'sp')), may hold values from 1 to 4
- gate_weight: bfloat16 [64, 4096, 1536], P('ep', None, 'sp'), may hold values from -0.09375 to 0.09375
- up_weight: bfloat16 [64, 4096, 1536], P('ep', None, 'sp'), may hold values from -0.09375 to 0.09375
- down_weight: bfloat16 [64, 1536, 4096], P('ep', 'sp'), may hold values from -0.15625 to 0.15625
Outputs:
- hidden_state: bfloat16 [32768, 4096], P(('ep', 'sp'))
- moe_out: bfloat16 [32768, 4096], P(('ep', 'sp'))
Inputs may be any that keep to these rules, and one draw needn't show every extreme that they name: `routes`: each row names 2 different experts. In each aligned block of 128 rows (the tokens of one device) no expert is named more than 5 times, and in some block some expert is named exactly 5 times.
All inputs are finite; a program needn't handle non-finite values.
Results may differ from a plain program's by a relative error of at most 0.019.
Values may be sent and summed in bfloat16 or wider, within the bound.
No kernel may reach another device: no remote copies, remote signals or barrier semaphores. Data moves between devices by JAX's collectives and lax.ppermute only.
A program may use at most 128 MiB of HBM per device.

v0:
```python
import jax
import jax.numpy as jnp
from jax import lax
from jax.sharding import PartitionSpec as P

D = 4096
HEADS = 32
KV_HEADS = 8
HEAD = 128
RANK = 32
epsilon = 1e-06


def rms_scale(inputs, gain_vec):
    widened = inputs.astype(jnp.float32)
    return (
        widened
        * lax.rsqrt(jnp.mean(widened * widened, axis=-1, keepdims=True) + epsilon)
        * gain_vec.astype(jnp.float32)
    )


def route_slots(block_routes, experts):
    flat_routes = block_routes.reshape(-1)
    matches = (flat_routes[:, None] == jnp.arange(experts, dtype=jnp.int32)[None, :]).astype(
        jnp.int32
    )
    earlier = jnp.cumsum(matches, axis=0) - matches
    return (flat_routes, jnp.sum(earlier * matches, axis=1))


def attention_block(
    stream_rows, base_rows, key_rows, value_rows, user_id, attention_gain, adapter_down, adapter_up
):
    normed = rms_scale(stream_rows, attention_gain).astype(jnp.bfloat16)
    down_cols = lax.dynamic_slice_in_dim(adapter_down, user_id * RANK, RANK, 1)
    up_cols = lax.dynamic_slice_in_dim(adapter_up, user_id * RANK, RANK, 1)
    low_rank = jnp.dot(normed, down_cols, preferred_element_type=jnp.float32).astype(jnp.bfloat16)
    adapter_delta = jnp.dot(low_rank, up_cols.T, preferred_element_type=jnp.float32)
    queries = (base_rows.astype(jnp.float32) + adapter_delta).astype(jnp.bfloat16)
    group_size = HEADS // KV_HEADS
    row_total = queries.shape[0]
    query_heads = queries.reshape(row_total, KV_HEADS, group_size, HEAD)
    key_split = key_rows.reshape(-1, KV_HEADS, HEAD)
    value_split = value_rows.reshape(-1, KV_HEADS, HEAD)
    scores = jnp.einsum(
        "qhgd,khd->hgqk", query_heads, key_split, preferred_element_type=jnp.float32
    ) * HEAD ** (-0.5)
    row_max = jnp.max(scores, axis=-1, keepdims=True)
    exponent = jnp.exp(scores - row_max)
    attn_probs = (exponent / jnp.sum(exponent, axis=-1, keepdims=True)).astype(jnp.bfloat16)
    attended = jnp.einsum(
        "hgqk,khd->qhgd", attn_probs, value_split, preferred_element_type=jnp.float32
    ).reshape(row_total, D)
    return (stream_rows.astype(jnp.float32) + attended).astype(jnp.bfloat16)


def on_device(
    stream,
    query_base,
    key_heads,
    value_heads,
    attention_gain,
    expert_gain,
    adapter_down,
    adapter_up,
    user_index,
    routes,
    route_weights,
    gate_weight,
    up_weight,
    down_weight,
):
    key_all, value_all, down_all, up_all = (
        lax.all_gather(key_heads, "sp", axis=0, tiled=True),
        lax.all_gather(value_heads, "sp", axis=0, tiled=True),
        lax.all_gather(adapter_down, "sp", axis=0, tiled=True),
        lax.all_gather(adapter_up, "sp", axis=0, tiled=True),
    )
    hidden_state = attention_block(
        stream, query_base, key_all, value_all, user_index[0], attention_gain, down_all, up_all
    )
    normed_moe = rms_scale(hidden_state, expert_gain).astype(jnp.bfloat16)
    tokens_dev = stream.shape[0]
    top_count = routes.shape[1]
    model_width = stream.shape[1]
    experts = lax.axis_size("ep")
    capacity = max(2, (5 * tokens_dev * top_count + 4 * experts - 1) // (4 * experts))
    own_routes = lax.dynamic_slice_in_dim(routes, lax.axis_index("sp") * tokens_dev, tokens_dev, 0)
    flat_routes, slot_index = route_slots(own_routes, experts)
    position = flat_routes * capacity + slot_index
    padded = jnp.concatenate([normed_moe, jnp.zeros((1, model_width), jnp.bfloat16)], axis=0)
    token_ids = jnp.arange(tokens_dev * top_count, dtype=jnp.int32) // top_count
    slot_table = jnp.full((experts * capacity,), tokens_dev, jnp.int32).at[position].set(token_ids)
    outgoing = padded[slot_table].reshape(experts, capacity, model_width)
    received = lax.all_to_all(outgoing, "ep", split_axis=0, concat_axis=0, tiled=True)
    arrived = lax.all_gather(received, "sp", axis=0, tiled=True)
    all_rows = arrived.reshape(-1, model_width)
    gate_local = gate_weight[0]
    up_local = up_weight[0]
    down_local = down_weight[0]
    gate_out = jnp.dot(all_rows, gate_local, preferred_element_type=jnp.float32)
    up_out = jnp.dot(all_rows, up_local, preferred_element_type=jnp.float32)
    activated = (jax.nn.silu(gate_out) * up_out).astype(jnp.bfloat16)
    summed = lax.psum_scatter(
        jnp.dot(activated, down_local, preferred_element_type=jnp.float32).astype(jnp.bfloat16),
        "sp",
        scatter_dimension=0,
        tiled=True,
    )
    expert_out = summed.reshape(experts, capacity, model_width)
    returned = lax.all_to_all(expert_out, "ep", split_axis=0, concat_axis=0, tiled=True)
    picked = returned.reshape(experts * capacity, model_width)[position].reshape(
        tokens_dev, top_count, model_width
    )
    route_share = route_weights.astype(jnp.float32)
    route_share = route_share / jnp.sum(route_share, axis=1, keepdims=True)
    moe_out = jnp.sum(picked.astype(jnp.float32) * route_share[:, :, None], axis=1).astype(
        jnp.bfloat16
    )
    return (hidden_state, moe_out)


def solution(mesh):
    in_specs = (
        P(("ep", "sp"), None),
        P(("ep", "sp"), None),
        P(("ep", "sp"), None),
        P(("ep", "sp"), None),
        P(),
        P(),
        P("sp", None),
        P("sp", None),
        P("ep"),
        P("ep", None),
        P(("ep", "sp"), None),
        P("ep", None, "sp"),
        P("ep", None, "sp"),
        P("ep", "sp", None),
    )
    out_specs = (P(("ep", "sp"), None), P(("ep", "sp"), None))
    return jax.shard_map(
        on_device, mesh=mesh, in_specs=in_specs, out_specs=out_specs, check_vma=False
    )
```

profile of v0, /device:TPU:8, one launch (start us, length us, event | category | flops | bytes accessed | tf_op | source)
XLA Modules:
  0.0 679.8 jit_solution(350134085212804269)
XLA Ops:
  7.2 0.0 copy-start
  7.2 0.0 copy-start.3
  7.2 0.0 all-gather.6.cloned.1.call-start
  7.2 0.7 all-gather.6.cloned.1.call-update
  7.9 0.0 all-gather.8.cloned.1.call-start
  8.0 0.7 all-gather.8.cloned.1.call-update
  8.7 0.0 all-gather.10.cloned.1.call-start
  8.7 1.8 copy.30
  10.5 0.0 all-gather.10.cloned.1.call-update
  10.6 0.0 all-gather.12.cloned.1.call-start
  10.6 0.5 all-gather.12.cloned.1.call-update
  11.1 0.0 all-gather.14.cloned.1.call-start
  11.2 0.7 broadcast_multiply_fusion
  11.9 0.1 copy.36
  12.0 0.1 eq.29
  12.1 0.1 eq.25
  12.9 0.6 reduce-window.6
  13.6 0.2 slice_reduce_fusion
  13.8 0.1 copy.35
  13.9 0.1 mul.109
  14.0 0.1 fusion.44
  14.2 1.4 scatter_custom_fusion
  15.6 0.7 convert_element_type.61
  16.3 1.5 fusion.21
  17.8 21.4 %all-gather.6.cloned.1.call-done = bf16[4096,128]{1,0:T(8,128)(2,1)} async-done(((bf16[1024,128]{1,0:T(8,128)(2,1)}), bf16[4096,128]{1,0:T(8,128)(2,1)}) %all-gather.6.cloned.1.call-update) | async-done | bytes 1048592 | tf_op jit(solution)/shard_map/all_gather | solution.py:77
  39.2 28.7 %all-gather.8.cloned.1.call-done = bf16[4096,128]{1,0:T(8,128)(2,1)} async-done(((bf16[1024,128]{1,0:T(8,128)(2,1)}), bf16[4096,128]{1,0:T(8,128)(2,1)}) %all-gather.8.cloned.1.call-update) | async-done | bytes 1048592 | tf_op jit(solution)/shard_map/all_gather | solution.py:78
  67.9 4.9 fusion.6
  72.8 3.0 reshape.101
  75.8 22.7 %all-gather.10.cloned.1.call-done = bf16[512,1024]{0,1:T(8,128)(2,1)} async-done(((bf16[128,1024]{0,1:T(8,128)(2,1)}), bf16[512,1024]{0,1:T(8,128)(2,1)}) %all-gather.10.cloned.1.call-update) | async-done | bytes 1048592 | tf_op jit(solution)/shard_map/all_gather | solution.py:75
  98.5 2.8 fusion.32
  101.3 3.2 copy-done.1
  104.5 2.4 fusion.60
  107.0 20.8 %all-gather.12.cloned.1.call-done = bf16[512,1024]{1,0:T(8,128)(2,1)} async-done(((bf16[128,1024]{1,0:T(8,128)(2,1)}), bf16[512,1024]{1,0:T(8,128)(2,1)}) %all-gather.12.cloned.1.call-update) | async-done | bytes 1048592 | tf_op jit(solution)/shard_map/all_gather | solution.py:76
  127.7 2.3 copy.33
  130.0 12.1 %fusion.8 = f32[8,4,128,128]{2,3,1,0:T(8,128)} fusion(bf16[512,8,128,1]{0,2,3,1:T(8,128)(2,1)} %bitcast.73, f32[8,4,128]{2,1,0:T(4,128)S(1)} %fusion.60, f32[8,128,4,512]{3,1,2,0:T(8,128)} %copy-done.1), kind=kOutput, calls=%fused_computation.15 | convolution fusion | flops 547361280 | bytes 11550720 | tf_op jit(solution)/shard_map/hgqk,khd->qhgd/dot_general | solution.py:52
  142.2 2.9 copy.34
  145.1 2.3 fusion.18
  147.3 0.0 copy-start.2
  147.4 1.0 copy-done.2
  148.3 0.3 fusion.20
  148.7 1.1 concatenate.3
  149.8 9.5 %gather_fusion = bf16[320,4096]{1,0:T(8,128)(2,1)} fusion(bf16[129,4096]{1,0:T(8,128)(2,1)} %concatenate.3, s32[1024]{0:T(1024)S(1)} %pad_clamp_fusion.1), kind=kCustom, calls=%fused_computation | custom fusion | bytes 5244160 | tf_op jit(solution)/shard_map/gather | solution.py:95
  159.3 4.7 reshape.106
  164.0 106.9 %all_to_all.10 = bf16[64,5,4096]{2,1,0:T(8,128)(2,1)S(1)} all-to-all(bf16[64,5,4096]{2,1,0:T(8,128)(2,1)} %reshape.106), channel_id=1, replica_groups=mesh['ep'=64,'sp'=4] {'ep'}, dimensions={0} | all-to-all | bytes 5242880 | tf_op jit(solution)/shard_map/all_to_all | solution.py:96
  270.9 3.2 copy.39
  274.1 0.0 all-gather.14.cloned.1.call-update
  274.1 0.0 reduce-scatter.2.cloned.1.call-start
  274.2 98.8 %all-gather.14.cloned.1.call-done = bf16[256,5,4096]{2,0,1:T(8,128)(2,1)} async-done(((bf16[64,5,4096]{2,0,1:T(8,128)(2,1)}), bf16[256,5,4096]{2,0,1:T(8,128)(2,1)}) %all-gather.14.cloned.1.call-update) | async-done | bytes 10485776 | tf_op jit(solution)/shard_map/all_gather | solution.py:97
  372.9 15.2 %copy.40 = bf16[256,5,4096]{2,1,0:T(8,128)(2,1)} copy(bf16[256,5,4096]{2,0,1:T(8,128)(2,1)} %all-gather.14.cloned.1.call-done) | data formatting | bytes 20971520 | tf_op jit(solution)/shard_map/all_gather | solution.py:97
  388.2 16.8 %reshape.107 = bf16[1280,4096]{1,0:T(8,128)(2,1)} reshape(bf16[256,5,4096]{2,1,0:T(8,128)(2,1)} %copy.40) | data formatting | bytes 20971520 | tf_op jit(solution)/shard_map/reshape | solution.py:98
  405.0 10.1 %fusion.11 = f32[1280,384]{1,0:T(8,128)} fusion(bf16[1280,4096]{1,0:T(8,128)(2,1)} %reshape.107, bf16[1,4096,384]{2,1,0:T(8,128)(2,1)} %param.25), kind=kOutput, calls=%fused_computation.19 | convolution fusion | flops 4026531840 | bytes 15597568 | tf_op jit(solution)/shard_map/dot_general | solution.py:102
  415.1 0.0 copy-done
  415.1 17.3 %convolution_convert_fusion = bf16[1280,4096]{1,0:T(8,128)(2,1)} fusion(bf16[1,384,4096]{2,1,0:T(8,128)(2,1)S(1)} %copy-done, bf16[1280,4096]{1,0:T(8,128)(2,1)} %reshape.107, bf16[1,4096,384]{2,1,0:T(8,128)(2,1)} %param.26, f32[1280,384]{1,0:T(8,128)} %fusion.11), kind=kOutput, calls=%fused_computation.4 | convolution fusion | flops 8061255680 | bytes 29229056 | tf_op jit(solution)/shard_map/dot_general | solution.py:106
  432.5 0.0 reduce-scatter.2.cloned.1.call-update
  432.5 101.2 %reduce-scatter.2.cloned.1.call-done = bf16[320,4096]{1,0:T(8,128)(2,1)} async-done(((bf16[1280,4096]{1,0:T(8,128)(2,1)}), bf16[320,4096]{1,0:T(8,128)(2,1)}) %reduce-scatter.2.cloned.1.call-update) | async-done | bytes 2621456 | tf_op jit(solution)/shard_map/reduce_scatter | solution.py:105
  533.7 4.7 reshape.108
  538.4 11.3 %all-to-all-start.1 = ((bf16[64,5,4096]{2,1,0:T(8,128)(2,1)}), bf16[64,5,4096]{2,1,0:T(8,128)(2,1)}, u32[]{:S(2)}, u32[]{:S(2)}) async-start(bf16[64,5,4096]{2,1,0:T(8,128)(2,1)} %reshape.108), calls=%async_computation.2 | async-start | bytes 8388608 | tf_op jit(solution)/shard_map/all_to_all | solution.py:112
  549.6 0.0 copy-done.4
  549.7 0.1 copy.41
  549.8 95.8 %all-to-all-done.1 = bf16[64,5,4096]{2,1,0:T(8,128)(2,1)} async-done(((bf16[64,5,4096]{2,1,0:T(8,128)(2,1)}), bf16[64,5,4096]{2,1,0:T(8,128)(2,1)}, u32[]{:S(2)}, u32[]{:S(2)}) %all-to-all-start.1) | async-done | bytes 2621472 | tf_op jit(solution)/shard_map/all_to_all | solution.py:112
  645.6 4.8 reshape.109
  650.3 7.4 %gather_fusion.1 = bf16[256,4096]{1,0:T(8,128)(2,1)} fusion(bf16[320,4096]{1,0:T(8,128)(2,1)} %reshape.109, s32[1024]{0:T(1024)S(1)} %pad_clamp_fusion), kind=kCustom, calls=%fused_computation.1 | custom fusion | bytes 4195328 | tf_op jit(solution)/shard_map/gather | solution.py:113
  657.7 5.4 reshape.110
  663.1 9.6 %multiply_reduce_fusion = bf16[128,4096]{1,0:T(8,128)(2,1)} fusion(f32[128,2,4096]{2,1,0:T(2,128)} %reshape.110, f32[128,2]{1,0:T(8,128)S(1)} %copy.41), kind=kLoop, calls=%fused_computation.13 | loop fusion | flops 1572864 | bytes 5243904 | tf_op jit(solution)/shard_map/reduce_sum | solution.py:118
  (16 shorter events, 0.1 us)
Async XLA Ops:
  7.2 408.0 %copy-start = (bf16[1,384,4096]{2,1,0:T(8,128)(2,1)S(1)}, bf16[1,384,4096]{2,1,0:T(8,128)(2,1)}, u32[]{:S(2)}) copy-start(bf16[1,384,4096]{2,1,0:T(8,128)(2,1)} %param.27) | copy-start | bytes 9437188
  7.2 10.6 %copy-start.3 = (bf16[4096]{0:T(1024)(128)(2,1)S(1)}, bf16[4096]{0:T(1024)(128)(2,1)}, u32[]{:S(2)}) copy-start(bf16[4096]{0:T(1024)(128)(2,1)} %param.19) | copy-start | bytes 24580
  7.2 32.1 %all-gather.6.cloned.1.call-start = ((), (), s32[]{:S(2)}) async-start(), calls=%async_computation.3 | async-start | bytes 1310720 | tf_op jit(solution)/shard_map/all_gather | solution.py:77
  7.9 60.0 %all-gather.8.cloned.1.call-start = ((), (), s32[]{:S(2)}) async-start(), calls=%async_computation.4 | async-start | bytes 1310720 | tf_op jit(solution)/shard_map/all_gather | solution.py:78
  8.7 89.9 %all-gather.10.cloned.1.call-start = ((), (), s32[]{:S(2)}) async-start(), calls=%async_computation.5 | async-start | bytes 1310720 | tf_op jit(solution)/shard_map/all_gather | solution.py:75
  10.6 117.2 %all-gather.12.cloned.1.call-start = ((), (), s32[]{:S(2)}) async-start(), calls=%async_computation.6 | async-start | bytes 1310720 | tf_op jit(solution)/shard_map/all_gather | solution.py:76
  11.1 361.8 %all-gather.14.cloned.1.call-start = ((), (), s32[]{:S(2)}) async-start(), calls=%async_computation.7 | async-start | bytes 13107200 | tf_op jit(solution)/shard_map/all_gather | solution.py:97
  101.3 3.2 copy-start.1
  147.3 1.0 copy-start.2
  274.1 259.5 %reduce-scatter.2.cloned.1.call-start = ((), (), s32[]{:S(2)}) async-start(), calls=%async_computation.8 | async-start | bytes 13107200 | tf_op jit(solution)/shard_map/reduce_scatter | solution.py:105
  538.3 11.3 %copy-start.4 = (s32[128,2]{0,1:T(2,128)S(1)}, s32[128,2]{0,1:T(2,128)}, u32[]{:S(2)}) copy-start(s32[128,2]{0,1:T(2,128)} %param.24) | copy-start | bytes 3076
  538.4 107.2 %all-to-all-start.1 = ((bf16[64,5,4096]{2,1,0:T(8,128)(2,1)}), bf16[64,5,4096]{2,1,0:T(8,128)(2,1)}, u32[]{:S(2)}, u32[]{:S(2)}) async-start(bf16[64,5,4096]{2,1,0:T(8,128)(2,1)} %reshape.108), calls=%async_computation.2 | async-start | bytes 8388608 | tf_op jit(solution)/shard_map/all_to_all | solution.py:112
Sparse Core Ops, SparseCore 0:
  9.8 29.3 all-gather.5
  41.0 26.8 all-gather.7
  69.7 28.7 all-gather.9
  100.2 27.5 all-gather.11
  274.2 98.6 all-gather.13
  432.6 101.0 reduce-scatter.1
where the time goes:
time: 685 us; the launch traced here: 680 us
  waiting for transfers between devices  391 us (57%)
  blocking collectives  107 us (16%)
  local copies, waits for them, and re-layouts  89.4 us (13%)
  matrix products  47.2 us (7%)
  other arithmetic  18.4 us (3%)
  between operations  15.2 us (2%)
  starting transfers between devices  11.5 us (2%)
    all_to_all x1, blocking collectives, on_device(): lax.all_to_all(outgoing, 'ep', split_axis=0, concat_axis=0, tiled=True)  107 us
    reduce_scatter x1, waiting for transfers between devices, on_device(): lax.psum_scatter(jnp.dot(activated, down_local, preferred_element_type=jn...  101 us
    all_gather x1, waiting for transfers between devices, on_device(): arrived = lax.all_gather(received, 'sp', axis=0, tiled=True)  98.8 us
    all_to_all x1, waiting for transfers between devices, on_device(): lax.all_to_all(expert_out, 'ep', split_axis=0, concat_axis=0, tiled=True)  95.8 us
    all_gather x1, waiting for transfers between devices, on_device(): lax.all_gather(adapter_up, 'sp', axis=0, tiled=True)  28.7 us
    all_gather x1, waiting for transfers between devices, on_device(): lax.all_gather(key_heads, 'sp', axis=0, tiled=True)  22.7 us
    all_gather x1, waiting for transfers between devices, on_device(): lax.all_gather(adapter_down, 'sp', axis=0, tiled=True)  21.4 us
    all_gather x1, waiting for transfers between devices, on_device(): lax.all_gather(value_heads, 'sp', axis=0, tiled=True)  20.8 us
  transfers between devices with their start and end apart: 7, of which 7 were waited for; matrix products, arithmetic and copies ran while one was open for 3% of the time, Pallas kernels for 0%

commit v1 on v0

--- a/solution.py
+++ b/solution.py
@@ -73,7 +73,9 @@
 ):
     key_all, value_all, down_all, up_all = (
         lax.all_gather(key_heads, "sp", axis=0, tiled=True),
-        lax.all_gather(value_heads, "sp", axis=0, tiled=True),
+        jnp.concatenate(
+            lax.all_to_all(jnp.stack([value_heads] * lax.axis_size("sp")), "sp", 0, 0), axis=0
+        ),
         lax.all_gather(adapter_down, "sp", axis=0, tiled=True),
         lax.all_gather(adapter_up, "sp", axis=0, tiled=True),
     )

time: 685 us -> 664 us (0.969)
  waiting for transfers between devices: 391 us -> 363 us
    all_gather x1 -> x0, waiting for transfers between devices: 20.8 us -> none  [on_device(): lax.all_gather(value_heads, 'sp', axis=0, tiled=True)]
    all_gather x1, waiting for transfers between devices: 21.4 us -> 1.99 us  [on_device(): lax.all_gather(adapter_down, 'sp', axis=0, tiled=True)]
    all_to_all x0 -> x1, waiting for transfers between devices: none -> 9.91 us  [on_device(): lax.all_to_all(jnp.stack([value_heads] * lax.axis_size('sp')), 'sp', 0, 0)]
where the time goes in v1:
time: 664 us; the launch traced here: 660 us
  waiting for transfers between devices  363 us (55%)
  blocking collectives  107 us (16%)
  local copies, waits for them, and re-layouts  95.1 us (14%)
  matrix products  47.2 us (7%)
  other arithmetic  17.7 us (3%)
  starting transfers between devices  15.7 us (2%)
  between operations  14.9 us (2%)
    all_to_all x1, blocking collectives, on_device(): lax.all_to_all(outgoing, 'ep', split_axis=0, concat_axis=0, tiled=True)  107 us
    reduce_scatter x1, waiting for transfers between devices, on_device(): lax.psum_scatter(jnp.dot(activated, down_local, preferred_element_type=jn...  101 us
    all_gather x1, waiting for transfers between devices, on_device(): arrived = lax.all_gather(received, 'sp', axis=0, tiled=True)  99.4 us
    all_to_all x1, waiting for transfers between devices, on_device(): lax.all_to_all(expert_out, 'ep', split_axis=0, concat_axis=0, tiled=True)  95.8 us
    all_gather x1, waiting for transfers between devices, on_device(): lax.all_gather(adapter_up, 'sp', axis=0, tiled=True)  29.8 us
    all_gather x1, waiting for transfers between devices, on_device(): lax.all_gather(key_heads, 'sp', axis=0, tiled=True)  23.1 us
    dot_general x1, matrix products, on_device(): jnp.dot(activated, down_local, preferred_element_type=jnp.float32)  17.3 us
    reshape x1, local copies, waits for them, and re-layouts, on_device(): all_rows = arrived.reshape(-1, model_width)  16.8 us
  transfers between devices with their start and end apart: 7, of which 7 were waited for; matrix products, arithmetic and copies ran while one was open for 3% of the time, Pallas kernels for 0%

profile of v1, /device:TPU:8, one launch (start us, length us, event | category | flops | bytes accessed | tf_op | source)
XLA Modules:
  0.0 660.0 jit_solution(14969424267927148718)
XLA Ops:
  7.2 0.0 copy-start
  7.2 0.0 copy-start.3
  7.2 0.0 copy-start.4
  7.2 0.0 all-gather.5.cloned.1.call-start
  7.2 0.7 all-gather.5.cloned.1.call-update
  7.9 0.0 all-gather.7.cloned.1.call-start
  8.0 0.7 all-gather.7.cloned.1.call-update
  8.7 1.1 copy.33
  9.8 1.1 stack.2
  10.9 4.3 all-to-all-start
  15.2 0.0 all-gather.9.cloned.1.call-start
  15.2 1.8 copy.30
  17.0 0.0 all-gather.9.cloned.1.call-update
  17.0 0.0 all-gather.11.cloned.1.call-start
  17.1 0.7 broadcast_multiply_fusion
  17.8 0.1 copy.37
  17.9 0.1 eq.29
  18.0 0.1 eq.25
  18.2 0.6 reduce-window.6
  18.8 0.2 slice_reduce_fusion
  19.0 0.1 copy.36
  19.2 0.1 mul.109
  19.3 0.1 fusion.45
  20.1 1.7 scatter_custom_fusion
  21.8 1.5 fusion.21
  23.4 9.9 %all-to-all-done = bf16[4,128,1024]{1,2,0:T(8,128)(2,1)} async-done(((bf16[4,128,1024]{1,2,0:T(8,128)(2,1)}), bf16[4,128,1024]{1,2,0:T(8,128)(2,1)}, u32[]{:S(2)}, u32[]{:S(2)}) %all-to-all-start) | async-done | bytes 1048608 | tf_op jit(solution)/shard_map/all_to_all | solution.py:77
  33.3 3.0 copy.34
  36.3 2.3 reshape.135
  38.5 2.0 all-gather.5.cloned.1.call-done
  40.5 29.8 %all-gather.7.cloned.1.call-done = bf16[4096,128]{1,0:T(8,128)(2,1)} async-done(((bf16[1024,128]{1,0:T(8,128)(2,1)}), bf16[4096,128]{1,0:T(8,128)(2,1)}) %all-gather.7.cloned.1.call-update) | async-done | bytes 1048592 | tf_op jit(solution)/shard_map/all_gather | solution.py:80
  70.4 4.9 fusion.6
  75.2 2.6 reshape.100
  77.8 23.1 %all-gather.9.cloned.1.call-done = bf16[512,1024]{0,1:T(8,128)(2,1)} async-done(((bf16[128,1024]{0,1:T(8,128)(2,1)}), bf16[512,1024]{0,1:T(8,128)(2,1)}) %all-gather.9.cloned.1.call-update) | async-done | bytes 1048592 | tf_op jit(solution)/shard_map/all_gather | solution.py:75
  100.9 2.8 fusion.33
  103.7 3.2 copy-done.1
  106.9 2.4 fusion.61
  109.4 12.1 %fusion.8 = f32[8,4,128,128]{2,3,1,0:T(8,128)} fusion(f32[8,4,128]{2,1,0:T(4,128)S(1)} %fusion.61, bf16[512,8,128,1]{0,2,1,3:T(8,128)(2,1)} %reshape.135, f32[8,128,4,512]{3,1,2,0:T(8,128)} %copy-done.1), kind=kOutput, calls=%fused_computation.15 | convolution fusion | flops 547361280 | bytes 11550720 | tf_op jit(solution)/shard_map/hgqk,khd->qhgd/dot_general | solution.py:52
  121.5 2.9 copy.35
  124.4 2.3 fusion.18
  126.7 0.0 copy-start.2
  126.7 1.0 copy-done.2
  127.7 0.3 fusion.20
  128.0 1.1 concatenate.3
  129.2 10.0 %gather_fusion = bf16[320,4096]{1,0:T(8,128)(2,1)} fusion(bf16[129,4096]{1,0:T(8,128)(2,1)} %concatenate.3, s32[1024]{0:T(1024)S(1)} %pad_clamp_fusion.1), kind=kCustom, calls=%fused_computation | custom fusion | bytes 5244160 | tf_op jit(solution)/shard_map/gather | solution.py:97
  139.1 4.7 reshape.104
  143.9 106.8 %all_to_all.15 = bf16[64,5,4096]{2,1,0:T(8,128)(2,1)S(1)} all-to-all(bf16[64,5,4096]{2,1,0:T(8,128)(2,1)} %reshape.104), channel_id=1, replica_groups=mesh['ep'=64,'sp'=4] {'ep'}, dimensions={0} | all-to-all | bytes 5242880 | tf_op jit(solution)/shard_map/all_to_all | solution.py:98
  250.6 3.2 copy.40
  253.8 0.0 all-gather.11.cloned.1.call-update
  253.9 0.0 reduce-scatter.2.cloned.1.call-start
  253.9 99.4 %all-gather.11.cloned.1.call-done = bf16[256,5,4096]{2,0,1:T(8,128)(2,1)} async-done(((bf16[64,5,4096]{2,0,1:T(8,128)(2,1)}), bf16[256,5,4096]{2,0,1:T(8,128)(2,1)}) %all-gather.11.cloned.1.call-update) | async-done | bytes 10485776 | tf_op jit(solution)/shard_map/all_gather | solution.py:99
  353.3 15.4 %copy.41 = bf16[256,5,4096]{2,1,0:T(8,128)(2,1)} copy(bf16[256,5,4096]{2,0,1:T(8,128)(2,1)} %all-gather.11.cloned.1.call-done) | data formatting | bytes 20971520 | tf_op jit(solution)/shard_map/all_gather | solution.py:99
  368.7 16.8 %reshape.105 = bf16[1280,4096]{1,0:T(8,128)(2,1)} reshape(bf16[256,5,4096]{2,1,0:T(8,128)(2,1)} %copy.41) | data formatting | bytes 20971520 | tf_op jit(solution)/shard_map/reshape | solution.py:100
  385.5 10.1 %fusion.11 = f32[1280,384]{1,0:T(8,128)} fusion(bf16[1280,4096]{1,0:T(8,128)(2,1)} %reshape.105, bf16[1,4096,384]{2,1,0:T(8,128)(2,1)} %param.25), kind=kOutput, calls=%fused_computation.19 | convolution fusion | flops 4026531840 | bytes 15597568 | tf_op jit(solution)/shard_map/dot_general | solution.py:104
  395.7 17.3 %convolution_convert_fusion = bf16[1280,4096]{1,0:T(8,128)(2,1)} fusion(bf16[1,384,4096]{2,1,0:T(8,128)(2,1)S(1)} %copy-done, bf16[1280,4096]{1,0:T(8,128)(2,1)} %reshape.105, bf16[1,4096,384]{2,1,0:T(8,128)(2,1)} %param.26, f32[1280,384]{1,0:T(8,128)} %fusion.11), kind=kOutput, calls=%fused_computation.4 | convolution fusion | flops 8061255680 | bytes 29229056 | tf_op jit(solution)/shard_map/dot_general | solution.py:108
  413.0 0.0 reduce-scatter.2.cloned.1.call-update
  413.0 101.2 %reduce-scatter.2.cloned.1.call-done = bf16[320,4096]{1,0:T(8,128)(2,1)} async-done(((bf16[1280,4096]{1,0:T(8,128)(2,1)}), bf16[320,4096]{1,0:T(8,128)(2,1)}) %reduce-scatter.2.cloned.1.call-update) | async-done | bytes 2621456 | tf_op jit(solution)/shard_map/reduce_scatter | solution.py:107
  514.2 4.7 reshape.106
  518.9 11.3 %all-to-all-start.2 = ((bf16[64,5,4096]{2,1,0:T(8,128)(2,1)}), bf16[64,5,4096]{2,1,0:T(8,128)(2,1)}, u32[]{:S(2)}, u32[]{:S(2)}) async-start(bf16[64,5,4096]{2,1,0:T(8,128)(2,1)} %reshape.106), calls=%async_computation.3 | async-start | bytes 8388608 | tf_op jit(solution)/shard_map/all_to_all | solution.py:114
  530.2 0.1 copy.42
  530.3 95.8 %all-to-all-done.2 = bf16[64,5,4096]{2,1,0:T(8,128)(2,1)} async-done(((bf16[64,5,4096]{2,1,0:T(8,128)(2,1)}), bf16[64,5,4096]{2,1,0:T(8,128)(2,1)}, u32[]{:S(2)}, u32[]{:S(2)}) %all-to-all-start.2) | async-done | bytes 2621472 | tf_op jit(solution)/shard_map/all_to_all | solution.py:114
  626.1 4.8 reshape.107
  630.9 7.4 %gather_fusion.1 = bf16[256,4096]{1,0:T(8,128)(2,1)} fusion(bf16[320,4096]{1,0:T(8,128)(2,1)} %reshape.107, s32[1024]{0:T(1024)S(1)} %pad_clamp_fusion), kind=kCustom, calls=%fused_computation.1 | custom fusion | bytes 4195328 | tf_op jit(solution)/shard_map/gather | solution.py:115
  638.2 5.4 reshape.108
  643.7 9.6 %multiply_reduce_fusion = bf16[128,4096]{1,0:T(8,128)(2,1)} fusion(f32[128,2,4096]{2,1,0:T(2,128)} %reshape.108, f32[128,2]{1,0:T(8,128)S(1)} %copy.42), kind=kLoop, calls=%fused_computation.13 | loop fusion | flops 1572864 | bytes 5243904 | tf_op jit(solution)/shard_map/reduce_sum | solution.py:120
  (20 shorter events, 0.1 us)
Async XLA Ops:
  7.2 388.5 %copy-start = (bf16[1,384,4096]{2,1,0:T(8,128)(2,1)S(1)}, bf16[1,384,4096]{2,1,0:T(8,128)(2,1)}, u32[]{:S(2)}) copy-start(bf16[1,384,4096]{2,1,0:T(8,128)(2,1)} %param.27) | copy-start | bytes 9437188
  7.2 12.9 %copy-start.3 = (bf16[4096]{0:T(1024)(128)(2,1)S(1)}, bf16[4096]{0:T(1024)(128)(2,1)}, u32[]{:S(2)}) copy-start(bf16[4096]{0:T(1024)(128)(2,1)} %param.18) | copy-start | bytes 24580
  7.2 12.9 %copy-start.4 = (bf16[4096]{0:T(1024)(128)(2,1)S(1)}, bf16[4096]{0:T(1024)(128)(2,1)}, u32[]{:S(2)}) copy-start(bf16[4096]{0:T(1024)(128)(2,1)} %param.19) | copy-start | bytes 24580
  7.2 33.3 %all-gather.5.cloned.1.call-start = ((), (), s32[]{:S(2)}) async-start(), calls=%async_computation.4 | async-start | bytes 1310720 | tf_op jit(solution)/shard_map/all_gather | solution.py:79
  7.9 62.4 %all-gather.7.cloned.1.call-start = ((), (), s32[]{:S(2)}) async-start(), calls=%async_computation.5 | async-start | bytes 1310720 | tf_op jit(solution)/shard_map/all_gather | solution.py:80
  10.9 22.4 %all-to-all-start = ((bf16[4,128,1024]{1,2,0:T(8,128)(2,1)}), bf16[4,128,1024]{1,2,0:T(8,128)(2,1)}, u32[]{:S(2)}, u32[]{:S(2)}) async-start(bf16[4,128,1024]{1,2,0:T(8,128)(2,1)} %stack.2), calls=%async_computation | async-start | bytes 2097152 | tf_op jit(solution)/shard_map/all_to_all | solution.py:77
  15.2 85.7 %all-gather.9.cloned.1.call-start = ((), (), s32[]{:S(2)}) async-start(), calls=%async_computation.6 | async-start | bytes 1310720 | tf_op jit(solution)/shard_map/all_gather | solution.py:75
  17.0 336.3 %all-gather.11.cloned.1.call-start = ((), (), s32[]{:S(2)}) async-start(), calls=%async_computation.7 | async-start | bytes 13107200 | tf_op jit(solution)/shard_map/all_gather | solution.py:99
  103.7 3.2 copy-start.1
  126.7 1.0 copy-start.2
  253.9 260.3 %reduce-scatter.2.cloned.1.call-start = ((), (), s32[]{:S(2)}) async-start(), calls=%async_computation.8 | async-start | bytes 13107200 | tf_op jit(solution)/shard_map/reduce_scatter | solution.py:107
  518.9 11.3 %copy-start.5 = (s32[128,2]{0,1:T(2,128)S(1)}, s32[128,2]{0,1:T(2,128)}, u32[]{:S(2)}) copy-start(s32[128,2]{0,1:T(2,128)} %param.24) | copy-start | bytes 3076
  518.9 107.2 %all-to-all-start.2 = ((bf16[64,5,4096]{2,1,0:T(8,128)(2,1)}), bf16[64,5,4096]{2,1,0:T(8,128)(2,1)}, u32[]{:S(2)}, u32[]{:S(2)}) async-start(bf16[64,5,4096]{2,1,0:T(8,128)(2,1)} %reshape.106), calls=%async_computation.3 | async-start | bytes 8388608 | tf_op jit(solution)/shard_map/all_to_all | solution.py:114
Sparse Core Ops, SparseCore 0:
  9.8 30.6 all-gather.4
  42.3 27.9 all-gather.6
  72.2 28.7 all-gather.8
  254.0 99.2 all-gather.10
  413.1 101.0 reduce-scatter.1
